TPU v7x, 32 devices: a whole 2x2x4 slice. The times are simulated.
32 devices in a mesh: mem: 2 (over x), col: 16 (over z, y, core).
Axes of the slice: x: 2, y: 2, z: 4, core: 2. Of those that a mesh axis runs over, the one named last changes fastest.
Arguments:
- perturbations: bfloat16 [2, 16, 384, 768], P('mem', None, 'col'), may hold values from -6 to 6
- gradient: float32 [16, 384, 768], P(None, 'col'), may hold values from -6 to 6
- member_weights: float32 [2], P('mem'), may hold values from 0.5 to 2
- scale_weights: float32 [3], replicated, may hold values from 0.2 to 2
- lon_filter: bfloat16 [3, 768, 768], P(None, 'mem'), may hold values from -1 to 1.5
- lat_filter: bfloat16 [3, 384, 384], P(None, 'col'), may hold values from -1 to 1.5
Outputs:
- increment: float32 [16, 384, 768], P('mem', 'col')
All inputs are finite; a program needn't handle non-finite values.
Results may differ from a plain program's by a relative error of at most 0.01.
Values may be sent and summed in bfloat16 or wider, within the bound.
A program may use at most 64 MiB of HBM per device.

v0:
```python
import jax
import jax.numpy as jnp
from jax import lax
from jax.sharding import PartitionSpec as P


def on_device(perturbations, gradient, member_weights, scale_weights, lon_filter, lat_filter):
    member = perturbations[0].astype(jnp.float32)
    schur = (member * gradient).astype(jnp.bfloat16)
    levels = lax.all_to_all(schur, "col", split_axis=0, concat_axis=1, tiled=True)
    along = jnp.einsum(
        "laj,sij->lsai",
        levels,
        lax.all_gather(lon_filter, "mem", axis=1, tiled=True),
        preferred_element_type=jnp.float32,
    ).astype(jnp.bfloat16)
    across = jnp.einsum(
        "sab,lsbi->lsai",
        lax.all_gather(lat_filter, "col", axis=1, tiled=True),
        along,
        preferred_element_type=jnp.float32,
    )
    filtered = jnp.einsum("s,lsai->lai", scale_weights, across).astype(jnp.bfloat16)
    back = lax.all_to_all(filtered, "col", split_axis=1, concat_axis=0, tiled=True)
    terms = member_weights[0] * member * back.astype(jnp.float32)
    return lax.psum_scatter(terms, "mem", scatter_dimension=0, tiled=True)


def solution(mesh):
    placed = (
        P("mem", None, "col", None),
        P(None, "col", None),
        P("mem"),
        P(),
        P(None, "mem", None),
        P(None, "col", None),
    )
    return jax.shard_map(
        on_device, mesh=mesh, in_specs=placed, out_specs=P("mem", "col", None), check_vma=False
    )
```

profile of v0, /device:TPU:0, one launch (start us, length us, event | category | flops | bytes accessed | tf_op | source)
XLA Modules:
  0.0 129.6 jit_solution(12170853550535788724)
XLA Ops:
  6.5 0.0 copy-start
  6.5 0.0 copy-start.1
  6.5 0.0 copy-start.2
  6.5 0.0 all-gather.2.cloned.1.call-start
  6.5 0.7 all-gather.2.cloned.1.call-update
  7.3 0.4 copy-done.1
  7.6 0.4 copy-done.2
  8.0 0.0 copy-start.3
  8.0 0.9 fusion.5
  8.9 7.4 %all-to-all-start = ((bf16[16,24,768]{2,1,0:T(8,128)(2,1)}), bf16[16,24,768]{2,1,0:T(8,128)(2,1)S(1)}, u32[]{:S(2)}, u32[]{:S(2)}) async-start(bf16[16,24,768]{2,1,0:T(8,128)(2,1)} %fusion.5), calls=%async_computation | async-start | bytes 1179648 | tf_op jit(solution)/shard_map/all_to_all | solution.py:10
  16.4 0.0 copy-done.3
  16.4 29.1 %all_gather.7 = bf16[3,384,384]{2,1,0:T(8,128)(2,1)S(1)} all-gather(bf16[3,24,384]{2,1,0:T(8,128)(2,1)S(1)} %copy-done.3), channel_id=1, replica_groups=mesh['mem'=2,'col'=16] {'col'}, dimensions={1}, use_global_device_ids=true | all-gather | bytes 940032 | tf_op jit(solution)/shard_map/all_gather | solution.py:19
  45.5 0.0 all-to-all-done
  45.5 15.5 %all-gather.2.cloned.1.call-done = bf16[3,768,768]{2,1,0:T(8,128)(2,1)} async-done(((bf16[3,384,768]{2,1,0:T(8,128)(2,1)}), bf16[3,768,768]{2,1,0:T(8,128)(2,1)}) %all-gather.2.cloned.1.call-update) | async-done | bytes 3538960 | tf_op jit(solution)/shard_map/all_gather | solution.py:14
  61.0 5.9 %convolution_bitcast_fusion = bf16[3,384,768]{1,2,0:T(8,128)(2,1)} fusion(bf16[3,384,384]{2,1,0:T(8,128)(2,1)S(1)} %all_gather.7, bf16[384,768,1]{1,0,2:T(8,128)(2,1)S(1)} %bitcast.56, bf16[3,768,768]{2,1,0:T(8,128)(2,1)} %all-gather.2.cloned.1.call-done), kind=kOutput, calls=%fused_computation | convolution fusion | flops 2039316480 | bytes 6782976 | tf_op jit(solution)/shard_map/sab,lsbi->lsai/dot_general | solution.py:17
  66.9 4.0 %copy.12 = bf16[3,384,768]{2,0,1:T(4,128)(2,1)S(1)} copy(bf16[3,384,768]{1,2,0:T(8,128)(2,1)} %convolution_bitcast_fusion) | data formatting | bytes 3538944 | tf_op jit(solution)/shard_map/reshape.6
  70.9 0.0 copy-done
  70.9 1.4 %fusion.10 = bf16[1,384,768]{2,0,1:T(2,128)(2,1)S(1)} fusion(bf16[3,384,768]{2,0,1:T(4,128)(2,1)S(1)} %copy.12, f32[3]{0:T(128)S(1)} %copy-done), kind=kOutput, calls=%fused_computation.13 | convolution fusion | flops 1769472 | bytes 2359308 | tf_op jit(solution)/shard_map/s,lsai->lai/dot_general | solution.py:23
  72.2 0.1 copy.19
  72.3 0.9 copy.20
  73.2 0.5 broadcast
  73.8 4.4 %reduce = bf16[384,768]{1,0:T(8,128)(2,1)S(1)} reduce(bf16[384,1,768]{2,1,0:T(2,128)(2,1)S(1)} %bitcast.54, bf16[]{:T(256)} %broadcast), dimensions={1}, to_apply=%bitcast.51.reduce_sub_computation | reduce | bytes 1179650
  78.1 1.0 reshape.33
  79.1 5.6 %all-to-all-start.1 = ((bf16[16,2,9216]{2,1,0:T(2,128)(2,1)}), bf16[16,2,9216]{2,1,0:T(2,128)(2,1)S(1)}, u32[]{:S(2)}, u32[]{:S(2)}) async-start(bf16[16,2,9216]{2,1,0:T(2,128)(2,1)} %reshape.33), calls=%async_computation.1 | async-start | bytes 1179648 | tf_op jit(solution)/shard_map/all_to_all | solution.py:24
  84.7 0.0 reduce-scatter.2.cloned.1.call-start
  85.4 14.7 %all-to-all-done.1 = bf16[16,2,9216]{2,1,0:T(2,128)(2,1)S(1)} async-done(((bf16[16,2,9216]{2,1,0:T(2,128)(2,1)}), bf16[16,2,9216]{2,1,0:T(2,128)(2,1)S(1)}, u32[]{:S(2)}, u32[]{:S(2)}) %all-to-all-start.1) | async-done | bytes 589856 | tf_op jit(solution)/shard_map/all_to_all | solution.py:24
  100.1 0.5 reshape.34
  100.6 0.1 copy.14
  100.7 1.2 fusion.4
  101.8 0.0 reduce-scatter.2.cloned.1.call-update
  101.9 20.9 %reduce-scatter.2.cloned.1.call-done = f32[8,24,768]{2,1,0:T(8,128)} async-done(((f32[16,24,768]{2,1,0:T(8,128)}), f32[8,24,768]{2,1,0:T(8,128)}) %reduce-scatter.2.cloned.1.call-update) | async-done | bytes 589840 | tf_op jit(solution)/shard_map/reduce_scatter | solution.py:26
Async XLA Ops:
  6.5 64.3 %copy-start = (f32[3]{0:T(128)S(1)}, f32[3]{0:T(128)}, u32[]{:S(2)}) copy-start(f32[3]{0:T(128)} %param.9) | copy-start | bytes 40
  6.5 1.1 copy-start.1
  6.5 1.5 %copy-start.2 = (f32[16,24,768]{2,1,0:T(8,128)S(1)}, f32[16,24,768]{2,1,0:T(8,128)}, u32[]{:S(2)}) copy-start(f32[16,24,768]{2,1,0:T(8,128)} %param.7) | copy-start | bytes 3538948
  6.5 54.4 %all-gather.2.cloned.1.call-start = ((), (), s32[]{:S(2)}) async-start(), calls=%async_computation.3 | async-start | bytes 5308416 | tf_op jit(solution)/shard_map/all_gather | solution.py:14
  8.0 8.4 %copy-start.3 = (bf16[3,24,384]{2,1,0:T(8,128)(2,1)S(1)}, bf16[3,24,384]{2,1,0:T(8,128)(2,1)}, u32[]{:S(2)}) copy-start(bf16[3,24,384]{2,1,0:T(8,128)(2,1)} %param.11) | copy-start | bytes 165892
  8.9 36.5 %all-to-all-start = ((bf16[16,24,768]{2,1,0:T(8,128)(2,1)}), bf16[16,24,768]{2,1,0:T(8,128)(2,1)S(1)}, u32[]{:S(2)}, u32[]{:S(2)}) async-start(bf16[16,24,768]{2,1,0:T(8,128)(2,1)} %fusion.5), calls=%async_computation | async-start | bytes 1179648 | tf_op jit(solution)/shard_map/all_to_all | solution.py:10
  79.1 21.0 %all-to-all-start.1 = ((bf16[16,2,9216]{2,1,0:T(2,128)(2,1)}), bf16[16,2,9216]{2,1,0:T(2,128)(2,1)S(1)}, u32[]{:S(2)}, u32[]{:S(2)}) async-start(bf16[16,2,9216]{2,1,0:T(2,128)(2,1)} %reshape.33), calls=%async_computation.1 | async-start | bytes 1179648 | tf_op jit(solution)/shard_map/all_to_all | solution.py:24
  84.7 38.0 %reduce-scatter.2.cloned.1.call-start = ((), (), s32[]{:S(2)}) async-start(), calls=%async_computation.4 | async-start | bytes 1769472 | tf_op jit(solution)/shard_map/reduce_scatter | solution.py:26
Sparse Core Ops, SparseCore 0:
  8.9 52.0 all-gather.1
  102.0 20.7 reduce-scatter.1
where the time goes:
time: 130 us
  waiting for transfers between devices  51.8 us (40%)
  blocking collectives  29.1 us (22%)
  between operations  14.1 us (11%)
  starting transfers between devices  13.1 us (10%)
  local copies, waits for them, and re-layouts  7.76 us (6%)
  matrix products  7.27 us (6%)
  other arithmetic  6.47 us (5%)
    all_gather x1, blocking collectives, on_device(): lax.all_gather(lat_filter, 'col', axis=1, tiled=True)  29.1 us
    reduce_scatter x1, waiting for transfers between devices, on_device(): return lax.psum_scatter(terms, 'mem', scatter_dimension=0, tiled=True)  20.9 us
    all_gather x1, waiting for transfers between devices, on_device(): lax.all_gather(lon_filter, 'mem', axis=1, tiled=True)  15.5 us
    all_to_all x1, waiting for transfers between devices, on_device(): lax.all_to_all(filtered, 'col', split_axis=1, concat_axis=0, tiled=True)  14.7 us
    all_to_all x1, starting transfers between devices, on_device(): lax.all_to_all(schur, 'col', split_axis=0, concat_axis=1, tiled=True)  7.41 us
    dot_general x1, matrix products, on_device(): jnp.einsum('sab,lsbi->lsai', lax.all_gather(lat_filter, 'col', axis=1, ti...  5.91 us
    all_to_all x1, starting transfers between devices, on_device(): lax.all_to_all(filtered, 'col', split_axis=1, concat_axis=0, tiled=True)  5.62 us
    unnamed x1, other arithmetic  4.37 us
  transfers between devices with their start and end apart: 4, of which 3 were waited for; matrix products, arithmetic and copies ran while one was open for 1% of the time, Pallas kernels for 0%

commit v1 on v0

--- a/solution.py
+++ b/solution.py
@@ -21,7 +21,10 @@
         preferred_element_type=jnp.float32,
     )
     filtered = jnp.einsum("s,lsai->lai", scale_weights, across).astype(jnp.bfloat16)
-    back = lax.all_to_all(filtered, "col", split_axis=1, concat_axis=0, tiled=True)
+    back = jnp.concatenate(
+        lax.all_to_all(jnp.stack(jnp.split(filtered, lax.axis_size("col"), axis=1)), "col", 0, 0),
+        axis=0,
+    )
     terms = member_weights[0] * member * back.astype(jnp.float32)
     return lax.psum_scatter(terms, "mem", scatter_dimension=0, tiled=True)
 

time: 130 us -> 133 us (1.023)
  local copies, waits for them, and re-layouts: 7.76 us -> 14.7 us
  other arithmetic: 6.47 us -> 2.11 us
    unnamed x12 -> x23, local copies, waits for them, and re-layouts: 2.8 us -> 10 us
    unnamed x1 -> x0, other arithmetic: 4.37 us -> none
    another operation x1 -> x2, local copies, waits for them, and re-layouts: 3.98 us -> 4.6 us
where the time goes in v1:
time: 133 us; the launch traced here: 132 us
  waiting for transfers between devices  51.8 us (39%)
  blocking collectives  29.1 us (22%)
  local copies, waits for them, and re-layouts  14.7 us (11%)
  between operations  14.1 us (11%)
  starting transfers between devices  13.1 us (10%)
  matrix products  7.27 us (5%)
  other arithmetic  2.11 us (2%)
    all_gather x1, blocking collectives, on_device(): lax.all_gather(lat_filter, 'col', axis=1, tiled=True)  29.1 us
    reduce_scatter x1, waiting for transfers between devices, on_device(): return lax.psum_scatter(terms, 'mem', scatter_dimension=0, tiled=True)  20.9 us
    all_gather x1, waiting for transfers between devices, on_device(): lax.all_gather(lon_filter, 'mem', axis=1, tiled=True)  15.5 us
    all_to_all x1, waiting for transfers between devices, on_device(): lax.all_to_all(jnp.stack(jnp.split(filtered, lax.axis_size('col'), axis=1...  14.7 us
    unnamed x23, local copies, waits for them, and re-layouts  10 us
    all_to_all x1, starting transfers between devices, on_device(): lax.all_to_all(schur, 'col', split_axis=0, concat_axis=1, tiled=True)  7.41 us
    dot_general x1, matrix products, on_device(): jnp.einsum('sab,lsbi->lsai', lax.all_gather(lat_filter, 'col', axis=1, ti...  5.91 us
    all_to_all x1, starting transfers between devices, on_device(): lax.all_to_all(jnp.stack(jnp.split(filtered, lax.axis_size('col'), axis=1...  5.62 us
  transfers between devices with their start and end apart: 4, of which 3 were waited for; matrix products, arithmetic and copies ran while one was open for 1% of the time, Pallas kernels for 0%

profile of v1, /device:TPU:0, one launch (start us, length us, event | category | flops | bytes accessed | tf_op | source)
XLA Modules:
  0.0 132.2 jit_solution(2582915562427774391)
XLA Ops:
  6.5 0.7 all-gather.2.cloned.1.call-update
  7.3 0.4 copy-done.1
  7.6 0.4 copy-done.2
  8.0 0.9 fusion.5
  8.9 7.4 %all-to-all-start = ((bf16[16,24,768]{2,1,0:T(8,128)(2,1)}), bf16[16,24,768]{2,1,0:T(8,128)(2,1)S(1)}, u32[]{:S(2)}, u32[]{:S(2)}) async-start(bf16[16,24,768]{2,1,0:T(8,128)(2,1)} %fusion.5), calls=%async_computation | async-start | bytes 1179648 | tf_op jit(solution)/shard_map/all_to_all | solution.py:10
  16.4 29.1 %all_gather.7 = bf16[3,384,384]{2,1,0:T(8,128)(2,1)S(1)} all-gather(bf16[3,24,384]{2,1,0:T(8,128)(2,1)S(1)} %copy-done.3), channel_id=1, replica_groups=mesh['mem'=2,'col'=16] {'col'}, dimensions={1}, use_global_device_ids=true | all-gather | bytes 940032 | tf_op jit(solution)/shard_map/all_gather | solution.py:19
  45.5 15.5 %all-gather.2.cloned.1.call-done = bf16[3,768,768]{2,1,0:T(8,128)(2,1)} async-done(((bf16[3,384,768]{2,1,0:T(8,128)(2,1)}), bf16[3,768,768]{2,1,0:T(8,128)(2,1)}) %all-gather.2.cloned.1.call-update) | async-done | bytes 3538960 | tf_op jit(solution)/shard_map/all_gather | solution.py:14
  61.0 5.9 %convolution_bitcast_fusion = bf16[3,384,768]{1,2,0:T(8,128)(2,1)} fusion(bf16[3,384,384]{2,1,0:T(8,128)(2,1)S(1)} %all_gather.7, bf16[384,768,1]{1,0,2:T(8,128)(2,1)S(1)} %bitcast.115, bf16[3,768,768]{2,1,0:T(8,128)(2,1)} %all-gather.2.cloned.1.call-done), kind=kOutput, calls=%fused_computation | convolution fusion | flops 2039316480 | bytes 6782976 | tf_op jit(solution)/shard_map/sab,lsbi->lsai/dot_general | solution.py:17
  66.9 4.0 %copy.25 = bf16[3,384,768]{2,0,1:T(4,128)(2,1)S(1)} copy(bf16[3,384,768]{1,2,0:T(8,128)(2,1)} %convolution_bitcast_fusion) | data formatting | bytes 3538944 | tf_op jit(solution)/shard_map/reshape.7
  70.9 1.4 %fusion.26 = bf16[1,384,768]{2,0,1:T(2,128)(2,1)S(1)} fusion(bf16[3,384,768]{2,0,1:T(4,128)(2,1)S(1)} %copy.25, f32[3]{0:T(128)S(1)} %copy-done), kind=kOutput, calls=%fused_computation.44 | convolution fusion | flops 1769472 | bytes 2359308 | tf_op jit(solution)/shard_map/s,lsai->lai/dot_general | solution.py:23
  72.3 0.1 copy.30
  72.3 0.6 fusion.22
  73.0 0.6 fusion.21
  73.6 0.6 fusion.20
  74.2 0.6 fusion.19
  74.8 0.6 fusion.18
  75.4 0.6 fusion.17
  76.0 0.6 fusion.16
  76.7 0.6 fusion.15
  77.3 0.6 fusion.14
  77.9 0.6 fusion.13
  78.5 0.6 fusion.12
  79.1 0.6 fusion.11
  79.8 0.6 fusion.10
  80.4 0.6 fusion.9
  81.0 0.6 fusion.8
  81.6 0.6 fusion.7
  82.2 5.6 %all-to-all-start.1 = ((bf16[16,1,24,768]{3,2,1,0:T(8,128)(2,1)}), bf16[16,1,24,768]{3,2,1,0:T(8,128)(2,1)S(1)}, u32[]{:S(2)}, u32[]{:S(2)}) async-start(bf16[16,1,24,768]{3,2,1,0:T(8,128)(2,1)} %fusion.7), calls=%async_computation.1 | async-start | bytes 1179648 | tf_op jit(solution)/shard_map/all_to_all | solution.py:25
  87.9 0.0 reduce-scatter.2.cloned.1.call-start
  88.6 14.7 %all-to-all-done.1 = bf16[16,1,24,768]{3,2,1,0:T(8,128)(2,1)S(1)} async-done(((bf16[16,1,24,768]{3,2,1,0:T(8,128)(2,1)}), bf16[16,1,24,768]{3,2,1,0:T(8,128)(2,1)S(1)}, u32[]{:S(2)}, u32[]{:S(2)}) %all-to-all-start.1) | async-done | bytes 589856 | tf_op jit(solution)/shard_map/all_to_all | solution.py:25
  103.2 1.2 fusion.4
  104.4 20.9 %reduce-scatter.2.cloned.1.call-done = f32[8,24,768]{2,1,0:T(8,128)} async-done(((f32[16,24,768]{2,1,0:T(8,128)}), f32[8,24,768]{2,1,0:T(8,128)}) %reduce-scatter.2.cloned.1.call-update) | async-done | bytes 589840 | tf_op jit(solution)/shard_map/reduce_scatter | solution.py:29
  (9 shorter events, 0.0 us)
Async XLA Ops:
  6.5 64.3 %copy-start = (f32[3]{0:T(128)S(1)}, f32[3]{0:T(128)}, u32[]{:S(2)}) copy-start(f32[3]{0:T(128)} %param.9) | copy-start | bytes 40
  6.5 1.1 copy-start.1
  6.5 1.5 %copy-start.2 = (f32[16,24,768]{2,1,0:T(8,128)S(1)}, f32[16,24,768]{2,1,0:T(8,128)}, u32[]{:S(2)}) copy-start(f32[16,24,768]{2,1,0:T(8,128)} %param.7) | copy-start | bytes 3538948
  6.5 54.4 %all-gather.2.cloned.1.call-start = ((), (), s32[]{:S(2)}) async-start(), calls=%async_computation.3 | async-start | bytes 5308416 | tf_op jit(solution)/shard_map/all_gather | solution.py:14
  8.0 8.4 %copy-start.3 = (bf16[3,24,384]{2,1,0:T(8,128)(2,1)S(1)}, bf16[3,24,384]{2,1,0:T(8,128)(2,1)}, u32[]{:S(2)}) copy-start(bf16[3,24,384]{2,1,0:T(8,128)(2,1)} %param.11) | copy-start | bytes 165892
  8.9 36.5 %all-to-all-start = ((bf16[16,24,768]{2,1,0:T(8,128)(2,1)}), bf16[16,24,768]{2,1,0:T(8,128)(2,1)S(1)}, u32[]{:S(2)}, u32[]{:S(2)}) async-start(bf16[16,24,768]{2,1,0:T(8,128)(2,1)} %fusion.5), calls=%async_computation | async-start | bytes 1179648 | tf_op jit(solution)/shard_map/all_to_all | solution.py:10
  82.2 21.0 %all-to-all-start.1 = ((bf16[16,1,24,768]{3,2,1,0:T(8,128)(2,1)}), bf16[16,1,24,768]{3,2,1,0:T(8,128)(2,1)S(1)}, u32[]{:S(2)}, u32[]{:S(2)}) async-start(bf16[16,1,24,768]{3,2,1,0:T(8,128)(2,1)} %fusion.7), calls=%async_computation.1 | async-start | bytes 1179648 | tf_op jit(solution)/shard_map/all_to_all | solution.py:25
  87.9 37.4 %reduce-scatter.2.cloned.1.call-start = ((), (), s32[]{:S(2)}) async-start(), calls=%async_computation.4 | async-start | bytes 1769472 | tf_op jit(solution)/shard_map/reduce_scatter | solution.py:29
Sparse Core Ops, SparseCore 0:
  8.9 52.0 all-gather.1
  104.6 20.7 reduce-scatter.1
